TPU v7x, 768 devices: a whole 4x8x12 slice. The times are simulated.
768 devices in a mesh: gx: 24 (over y, z_hi), gy: 16 (over z_lo, x), gz: 2 (over core).
Axes of the slice: x: 4, y: 8, z: 12 (z_hi: 3, z_lo: 4; z = z_hi * 4 + z_lo), core: 2. Of those that a mesh axis runs over, the one named last changes fastest.
Arguments:
- layer_east: float32 [16, 2048, 3072], P('gz', 'gy', 'gx'), may hold values from -6 to 6
- layer_north: float32 [16, 2048, 3072], P('gz', 'gy', 'gx'), may hold values from -6 to 6
- layer_press: float32 [16, 2048, 3072], P('gz', 'gy', 'gx'), may hold values from -6 to 6
- surface: float32 [2048, 3072], P('gy', 'gx'), may hold values from -3 to 3
- land_sea: int32 [2048, 3072], P('gy', 'gx'), may hold values 0 or 1
- bottom_level: int32 [2048, 3072], P('gy', 'gx'), may hold values from 12 to 16
- coriolis: float32 [2048, 3072], P('gy', 'gx'), may hold values from -1 to 1
- level_thick: float32 [16], P('gz'), may hold values from 0.25 to 0.3
Outputs:
- surface_next: float32 [2048, 3072], P('gy', 'gx')
- east_next: float32 [16, 2048, 3072], P('gz', 'gy', 'gx')
- north_next: float32 [16, 2048, 3072], P('gz', 'gy', 'gx')
All inputs are finite; a program needn't handle non-finite values. No bound on the sum of `land_sea` on one device may be relied on, other than what follows from the above.
Results may differ from a plain program's by a relative error of at most 0.00002.
Values sent between devices are 32-bit elements; how exact they have to be, the bound alone decides.
A program may use at most 32 MiB of HBM per device.

v0:
```python
import jax
import jax.numpy as jnp
from jax import lax
from jax.sharding import PartitionSpec as P

SUBSTEPS = 4


COURANT = 0.25
VISCOSITY = 0.1


def with_halo(x, sides, width):
    edges = {}
    for axis, dim in sides:
        count, length = (lax.axis_size(axis), x.shape[dim])
        up = [(i, (i + 1) % count) for i in range(count)]
        last = lax.slice_in_dim(x, length - width, length, axis=dim)
        initial = lax.slice_in_dim(x, 0, width, axis=dim)
        edges[dim] = (
            lax.ppermute(last, axis, up),
            lax.ppermute(initial, axis, [(b, a) for a, b in up]),
        )
    done = []
    for _, dim in sides:
        low, high = edges[dim]
        around = [(width, width) if d in done else (0, 0) for d in range(x.ndim)]
        x = jnp.concatenate([jnp.pad(low, around), x, jnp.pad(high, around)], axis=dim)
        done.append(dim)
    return x


def copy_for_each(x, axis):
    count = lax.axis_size(axis)
    return lax.all_to_all(jnp.broadcast_to(x[None], (count, *x.shape)), axis, 0, 0, tiled=True)


def taken_together(x, axis):
    return copy_for_each(x, axis).sum(axis=0)


def extended(block, sides, width):
    for axis, dim in sides:
        count = lax.axis_size(axis)
        forward = [(i, i + 1) for i in range(count - 1)]
        forward.append((count - 1, 0))
        backward = [(target, source) for source, target in forward]
        low = lax.ppermute(
            lax.slice_in_dim(block, block.shape[dim] - width, None, axis=dim), axis, forward
        )
        high = lax.ppermute(lax.slice_in_dim(block, 0, width, axis=dim), axis, backward)
        block = jnp.concatenate([low, block, high], axis=dim)
    return block


def layer_terms(centre, east, west, north, south, coriolis):
    vel_east, vel_north, press, active = centre
    grad_x = 0.5 * (east[3] * (east[2] - press) + west[3] * (press - west[2]))
    grad_y = 0.5 * (north[3] * (north[2] - press) + south[3] * (press - south[2]))

    def friction(slot, value):
        return (
            east[3] * (east[slot] - value)
            + west[3] * (west[slot] - value)
            + north[3] * (north[slot] - value)
            + south[3] * (south[slot] - value)
        )

    tend_east = active * (-grad_x + coriolis * vel_north + VISCOSITY * friction(0, vel_east))
    tend_north = active * (-grad_y - coriolis * vel_east + VISCOSITY * friction(1, vel_north))
    return (tend_east, tend_north)


def surface_step(
    height, trans_east, trans_north, ocean_mid, depth, coriolis, force_east, force_north
):
    spread = 0.5 * (trans_east[1:-1, 2:] - trans_east[1:-1, :-2]) + 0.5 * (
        trans_north[2:, 1:-1] - trans_north[:-2, 1:-1]
    )
    height_mid = ocean_mid * (height[1:-1, 1:-1] - COURANT * spread)
    slope_x = 0.5 * (height_mid[1:-1, 2:] - height_mid[1:-1, :-2])
    slope_y = 0.5 * (height_mid[2:, 1:-1] - height_mid[:-2, 1:-1])
    ocean_core = ocean_mid[1:-1, 1:-1]
    old_east = trans_east[2:-2, 2:-2]
    old_north = trans_north[2:-2, 2:-2]
    new_east = ocean_core * (
        old_east + COURANT * (-depth * slope_x + coriolis * old_north + force_east)
    )
    new_north = ocean_core * (
        old_north + COURANT * (-depth * slope_y - coriolis * old_east + force_north)
    )
    return (height_mid, new_east, new_north)


def cropped(field, margin):
    return field[..., margin : field.shape[-2] - margin, margin : field.shape[-1] - margin]


def on_device(
    layer_east, layer_north, layer_press, surface, land_sea, bottom_level, coriolis, level_thick
):
    levels = layer_east.shape[0]
    ocean = land_sea.astype(jnp.float32)
    deepest = ocean * bottom_level.astype(jnp.float32)
    stacked = jnp.concatenate([layer_east, layer_north, layer_press, deepest[None]], axis=0)
    widened = with_halo(stacked, (("gx", 2), ("gy", 1)), 1)
    indices = (lax.axis_index("gz") * levels + jnp.arange(levels)).astype(jnp.float32)[
        :, None, None
    ]
    wide_deepest = widened[3 * levels]
    wide_active = (indices < wide_deepest[None]).astype(jnp.float32)
    fields = (
        widened[:levels],
        widened[levels : 2 * levels],
        widened[2 * levels : 3 * levels],
        wide_active,
    )
    centre = tuple((item[:, 1:-1, 1:-1] for item in fields))
    east = tuple((item[:, 1:-1, 2:] for item in fields))
    west = tuple((item[:, 1:-1, :-2] for item in fields))
    north = tuple((item[:, 2:, 1:-1] for item in fields))
    south = tuple((item[:, :-2, 1:-1] for item in fields))
    active = centre[3]
    tend_east, tend_north = layer_terms(centre, east, west, north, south, coriolis)
    thick = level_thick[:, None, None]
    masked_east = active * layer_east
    masked_north = active * layer_north
    partial_sums = jnp.stack(
        [
            jnp.sum(thick * tend_east, axis=0),
            jnp.sum(thick * tend_north, axis=0),
            jnp.sum(thick * masked_east, axis=0),
            jnp.sum(thick * masked_north, axis=0),
            jnp.sum(thick * active, axis=0),
        ]
    )
    totals = taken_together(partial_sums, "gz")
    force_east, force_north, sum_east, sum_north, depth = (
        totals[0],
        totals[1],
        totals[2],
        totals[3],
        totals[4],
    )
    reach = 2 * SUBSTEPS
    state = jnp.stack(
        [surface, sum_east, sum_north, force_east, force_north, depth, coriolis, ocean]
    )
    region = extended(state, (("gx", 2), ("gy", 1)), reach)
    height, trans_east, trans_north = (region[0], region[1], region[2])
    for step in range(SUBSTEPS):
        ocean_mid = cropped(region[7], 2 * step + 1)
        statics = cropped(region[3:7], 2 * step + 2)
        height_mid, trans_east, trans_north = surface_step(
            height,
            trans_east,
            trans_north,
            ocean_mid,
            statics[2],
            statics[3],
            statics[0],
            statics[1],
        )
        height = height_mid[1:-1, 1:-1]
    timestep = SUBSTEPS * COURANT
    floor_depth = depth + (1.0 - ocean)
    east_next = active * (
        masked_east
        + timestep * tend_east
        + (trans_east - sum_east - timestep * force_east) / floor_depth
    )
    north_next = active * (
        masked_north
        + timestep * tend_north
        + (trans_north - sum_north - timestep * force_north) / floor_depth
    )
    return (height, east_next, north_next)


def solution(mesh):
    return jax.shard_map(
        on_device,
        mesh=mesh,
        in_specs=(
            P("gz", "gy", "gx"),
            P("gz", "gy", "gx"),
            P("gz", "gy", "gx"),
            P("gy", "gx"),
            P("gy", "gx"),
            P("gy", "gx"),
            P("gy", "gx"),
            P("gz"),
        ),
        out_specs=(P("gy", "gx"), P("gz", "gy", "gx"), P("gz", "gy", "gx")),
        check_vma=False,
    )
```

profile of v0, /device:TPU:1, one launch (start us, length us, event | category | flops | bytes accessed | tf_op | source)
XLA Modules:
  0.0 128.1 jit_solution(1852497133691647529)
XLA Ops:
  0.6 0.9 multiply_bitcast_fusion
  1.5 1.5 %pad_maximum_fusion = f32[25,128,128]{2,1,0:T(8,128)S(1)} fusion(f32[1,128,128]{2,1,0:T(8,128)S(1)} %multiply_bitcast_fusion, f32[8,128,128]{2,1,0:T(8,128)} %param.10, f32[8,128,128]{2,1,0:T(8,128)} %param.9, f32[8,128,128]{2,1,0:T(8,128)} %param.8), kind=kLoop, calls=%fused_computation.2 | loop fusion | flops 1228800 | bytes 3276800 | tf_op jit(solution)/shard_map/concatenate | solution.py:105
  3.0 1.8 %fusion.122 = (f32[25,128,1]{2,1,0:T(8,128)}, f32[25,128,1]{2,1,0:T(8,128)S(1)}) fusion(f32[25,128,128]{2,1,0:T(8,128)S(1)} %pad_maximum_fusion), kind=kLoop, calls=%fused_computation.223 | loop fusion | bytes 51200 | tf_op jit(solution)/shard_map/slice | solution.py:18
  4.8 2.2 %copy.46 = f32[25,128,1]{1,0,2:T(8,128)S(1)} copy(f32[25,128,1]{2,1,0:T(8,128)} %get-tuple-element.19) | data formatting | bytes 25600 | tf_op jit(solution)/shard_map/slice | solution.py:18
  7.0 11.5 %collective-permute-start.1 = (f32[25,128,1]{1,0,2:T(8,128)S(1)}, f32[25,128,1]{1,0,2:T(8,128)S(1)}, u32[]{:S(2)}, u32[]{:S(2)}) collective-permute-start(f32[25,128,1]{1,0,2:T(8,128)S(1)} %copy.46), channel_id=1, source_target_pairs={{0,32},{32,64},{64,96},{96,128},{128,160},{160,192},{192,224},{224... | collective-permute-start | bytes 38408 | tf_op jit(solution)/shard_map/ppermute | solution.py:21
  18.4 0.0 copy-start.12
  18.5 0.6 copy.47
  19.1 8.5 %collective-permute-start.2 = (f32[25,128,1]{1,0,2:T(8,128)S(1)}, f32[25,128,1]{1,0,2:T(8,128)S(1)}, u32[]{:S(2)}, u32[]{:S(2)}) collective-permute-start(f32[25,128,1]{1,0,2:T(8,128)S(1)} %copy.47), channel_id=1, source_target_pairs={{32,0},{64,32},{96,64},{128,96},{160,128},{192,160},{224,192},{256... | collective-permute-start | bytes 38408 | tf_op jit(solution)/shard_map/ppermute | solution.py:22
  27.6 3.1 %collective-permute-start = (f32[25,1,128]{2,1,0:T(1,128)S(1)}, f32[25,1,128]{2,1,0:T(1,128)S(1)}, u32[]{:S(2)}, u32[]{:S(2)}) collective-permute-start(f32[25,1,128]{2,1,0:T(1,128)S(1)} %get-tuple-element.21), channel_id=1, source_target_pairs={{0,2},{2,4},{4,6},{6,8},{8,10},{10,12},{12,14},{14,16},{16,18},{18... | collective-permute-start | bytes 38408 | tf_op jit(solution)/shard_map/ppermute | solution.py:21
  30.7 6.1 %collective-permute-start.3 = (f32[25,1,128]{2,1,0:T(1,128)S(1)}, f32[25,1,128]{2,1,0:T(1,128)S(1)}, u32[]{:S(2)}, u32[]{:S(2)}) collective-permute-start(f32[25,1,128]{2,1,0:T(1,128)S(1)} %get-tuple-element.22), channel_id=1, source_target_pairs={{2,0},{4,2},{6,4},{8,6},{10,8},{12,10},{14,12},{16,14},{18,16},{20... | collective-permute-start | bytes 38408 | tf_op jit(solution)/shard_map/ppermute | solution.py:22
  36.8 0.6 bitcast_dynamic-update-slice_fusion.7
  37.5 0.5 copy.48
  38.0 1.7 %copy.49 = f32[25,128,1]{2,1,0:T(8,128)} copy(f32[25,128,1]{1,0,2:T(8,128)S(1)} %collective-permute-done.2) | data formatting | bytes 25600 | tf_op jit(solution)/shard_map/ppermute | solution.py:22
  39.7 0.1 pad.7
  39.9 0.1 pad.8
  40.0 0.0 copy-start.3
  40.0 0.0 copy-start.7
  40.0 0.0 copy-start.10
  40.0 0.0 copy-start.13
  40.0 1.1 fusion.99
  41.2 0.1 compare_convert_fusion
  41.3 0.1 copy-done
  41.5 0.1 copy-done.3
  41.6 0.2 copy-done.7
  41.7 7.8 %multiply_reduce_fusion = (f32[128,128]{1,0:T(8,128)S(1)}, f32[128,128]{1,0:T(8,128)S(1)}, f32[128,128]{1,0:T(8,128)S(1)}, f32[128,128]{1,0:T(8,128)S(1)}, f32[1...) fusion(f32[8,130,130]{2,1,0:T(8,128)S(1)} %compare_convert_fusion, f32[8]{0:T(128)S(1)} %copy-done.13, ...), kind=kLoop, calls=%fused_computation.71 | loop fusion | flops 15384576 | bytes 5753264 | tf_op jit(solution)/shard_map/reduce_sum | solution.py:134
  49.7 0.0 copy-start.11
  49.7 7.0 %all_to_all.5 = f32[2,5,128,128]{3,2,1,0:T(8,128)S(1)} all-to-all(f32[2,5,128,128]{3,2,1,0:T(8,128)S(1)} %broadcast_in_dim.7), channel_id=1, replica_groups=mesh['gx'=24,'gy'=16,'gz'=2] {'gz'}, dimensions={0} | all-to-all | bytes 1310720 | tf_op jit(solution)/shard_map/all_to_all | solution.py:35
  56.8 0.2 fusion.123
  57.0 1.9 %collective-permute-start.4 = (f32[8,128,8]{2,1,0:T(8,128)S(1)}, f32[8,128,8]{2,1,0:T(8,128)S(1)}, u32[]{:S(2)}, u32[]{:S(2)}) collective-permute-start(f32[8,128,8]{2,1,0:T(8,128)S(1)} %get-tuple-element.33), channel_id=1, source_target_pairs={{0,32},{32,64},{64,96},{96,128},{128,160},{160,192},{192,224},{224... | collective-permute-start | bytes 98312 | tf_op jit(solution)/shard_map/ppermute | solution.py:48
  58.9 9.4 %collective-permute-start.5 = (f32[8,128,8]{2,1,0:T(8,128)S(1)}, f32[8,128,8]{2,1,0:T(8,128)S(1)}, u32[]{:S(2)}, u32[]{:S(2)}) collective-permute-start(f32[8,128,8]{2,1,0:T(8,128)S(1)} %get-tuple-element.34), channel_id=1, source_target_pairs={{32,0},{64,32},{96,64},{128,96},{160,128},{192,160},{224,192},{256... | collective-permute-start | bytes 98312 | tf_op jit(solution)/shard_map/ppermute | solution.py:51
  68.3 44.1 %collective-permute-done.4 = f32[8,128,8]{2,1,0:T(8,128)S(1)} collective-permute-done((f32[8,128,8]{2,1,0:T(8,128)S(1)}, f32[8,128,8]{2,1,0:T(8,128)S(1)}, u32[]{:S(2)}, u32[]{:S(2)}) %collective-permute-start.4) | collective-permute-done | bytes 32800 | tf_op jit(solution)/shard_map/ppermute | solution.py:48
  112.5 0.1 pad_maximum_fusion.29
  112.6 1.9 %collective-permute-start.6 = (f32[8,8,144]{2,1,0:T(8,128)S(1)}, f32[8,8,144]{2,1,0:T(8,128)S(1)}, u32[]{:S(2)}, u32[]{:S(2)}) collective-permute-start(f32[8,8,144]{2,1,0:T(8,128)S(1)} %get-tuple-element.23), channel_id=1, source_target_pairs={{0,2},{2,4},{4,6},{6,8},{8,10},{10,12},{12,14},{14,16},{16,18},{18... | collective-permute-start | bytes 110600 | tf_op jit(solution)/shard_map/ppermute | solution.py:48
  114.5 7.3 %collective-permute-start.7 = (f32[8,8,144]{2,1,0:T(8,128)S(1)}, f32[8,8,144]{2,1,0:T(8,128)S(1)}, u32[]{:S(2)}, u32[]{:S(2)}) collective-permute-start(f32[8,8,144]{2,1,0:T(8,128)S(1)} %get-tuple-element.24), channel_id=1, source_target_pairs={{2,0},{4,2},{6,4},{8,6},{10,8},{12,10},{14,12},{16,14},{18,16},{20... | collective-permute-start | bytes 110600 | tf_op jit(solution)/shard_map/ppermute | solution.py:51
  121.8 1.3 %collective-permute-done.7 = f32[8,8,144]{2,1,0:T(8,128)S(1)} collective-permute-done((f32[8,8,144]{2,1,0:T(8,128)S(1)}, f32[8,8,144]{2,1,0:T(8,128)S(1)}, u32[]{:S(2)}, u32[]{:S(2)}) %collective-permute-start.7) | collective-permute-done | bytes 36896 | tf_op jit(solution)/shard_map/ppermute | solution.py:51
  123.1 0.5 pad_maximum_fusion.1
  123.6 0.3 fusion.58
  123.9 0.5 fusion.50
  124.4 0.3 fusion.39
  124.6 0.4 fusion.94
  125.1 0.2 fusion.83
  125.3 0.0 copy-start.4
  125.3 0.0 copy-start.8
  125.3 0.0 copy-start.9
  125.4 0.4 fusion.75
  125.8 0.3 fusion.64
  126.1 0.8 fusion.102
  126.9 1.3 add_multiply_fusion
  (37 shorter events, 0.3 us)
Async XLA Ops:
  4.8 22.7 %copy-start.1 = (f32[8,128,128]{2,1,0:T(8,128)S(1)}, f32[8,128,128]{2,1,0:T(8,128)}, u32[]{:S(2)}) copy-start(f32[8,128,128]{2,1,0:T(8,128)} %param.9) | copy-start | bytes 1572868
  4.8 22.7 %copy-start.2 = (f32[8,128,128]{2,1,0:T(8,128)S(1)}, f32[8,128,128]{2,1,0:T(8,128)}, u32[]{:S(2)}) copy-start(f32[8,128,128]{2,1,0:T(8,128)} %param.8) | copy-start | bytes 1572868
  4.8 22.7 %copy-start.6 = (f32[8,128,128]{2,1,0:T(8,128)S(1)}, f32[8,128,128]{2,1,0:T(8,128)}, u32[]{:S(2)}) copy-start(f32[8,128,128]{2,1,0:T(8,128)} %param.10) | copy-start | bytes 1572868
  7.0 30.5 %collective-permute-start.1 = (f32[25,128,1]{1,0,2:T(8,128)S(1)}, f32[25,128,1]{1,0,2:T(8,128)S(1)}, u32[]{:S(2)}, u32[]{:S(2)}) collective-permute-start(f32[25,128,1]{1,0,2:T(8,128)S(1)} %copy.46), channel_id=1, source_target_pairs={{0,32},{32,64},{64,96},{96,128},{128,160},{160,192},{192,224},{224... | collective-permute-start | bytes 38408 | tf_op jit(solution)/shard_map/ppermute | solution.py:21
  18.4 18.4 %copy-start.12 = (f32[128,128]{1,0:T(8,128)S(1)}, f32[128,128]{1,0:T(8,128)}, u32[]{:S(2)}) copy-start(f32[128,128]{1,0:T(8,128)} %param.11) | copy-start | bytes 196612
  19.1 18.9 %collective-permute-start.2 = (f32[25,128,1]{1,0,2:T(8,128)S(1)}, f32[25,128,1]{1,0,2:T(8,128)S(1)}, u32[]{:S(2)}, u32[]{:S(2)}) collective-permute-start(f32[25,128,1]{1,0,2:T(8,128)S(1)} %copy.47), channel_id=1, source_target_pairs={{32,0},{64,32},{96,64},{128,96},{160,128},{192,160},{224,192},{256... | collective-permute-start | bytes 38408 | tf_op jit(solution)/shard_map/ppermute | solution.py:22
  27.6 12.1 %collective-permute-start = (f32[25,1,128]{2,1,0:T(1,128)S(1)}, f32[25,1,128]{2,1,0:T(1,128)S(1)}, u32[]{:S(2)}, u32[]{:S(2)}) collective-permute-start(f32[25,1,128]{2,1,0:T(1,128)S(1)} %get-tuple-element.21), channel_id=1, source_target_pairs={{0,2},{2,4},{4,6},{6,8},{8,10},{10,12},{12,14},{14,16},{16,18},{18... | collective-permute-start | bytes 38408 | tf_op jit(solution)/shard_map/ppermute | solution.py:21
  30.7 9.1 %collective-permute-start.3 = (f32[25,1,128]{2,1,0:T(1,128)S(1)}, f32[25,1,128]{2,1,0:T(1,128)S(1)}, u32[]{:S(2)}, u32[]{:S(2)}) collective-permute-start(f32[25,1,128]{2,1,0:T(1,128)S(1)} %get-tuple-element.22), channel_id=1, source_target_pairs={{2,0},{4,2},{6,4},{8,6},{10,8},{12,10},{14,12},{16,14},{18,16},{20... | collective-permute-start | bytes 38408 | tf_op jit(solution)/shard_map/ppermute | solution.py:22
  40.0 1.5 %copy-start = (f32[25,128,1]{2,1,0:T(8,128)S(1)}, f32[25,128,1]{2,1,0:T(8,128)}, u32[]{:S(2)}) copy-start(f32[25,128,1]{2,1,0:T(8,128)} %copy.49) | copy-start | bytes 38404
  40.0 1.6 %copy-start.3 = (f32[8,128,128]{2,1,0:T(8,128)S(1)}, f32[8,128,128]{2,1,0:T(8,128)}, u32[]{:S(2)}) copy-start(f32[8,128,128]{2,1,0:T(8,128)} %param.8) | copy-start | bytes 1572868
  40.0 1.7 %copy-start.7 = (f32[8,128,128]{2,1,0:T(8,128)S(1)}, f32[8,128,128]{2,1,0:T(8,128)}, u32[]{:S(2)}) copy-start(f32[8,128,128]{2,1,0:T(8,128)} %param.10) | copy-start | bytes 1572868
  40.0 1.7 %copy-start.10 = (f32[128,128]{1,0:T(8,128)S(1)}, f32[128,128]{1,0:T(8,128)}, u32[]{:S(2)}) copy-start(f32[128,128]{1,0:T(8,128)} %param.14) | copy-start | bytes 196612
  40.0 1.7 %copy-start.13 = (f32[8]{0:T(128)S(1)}, f32[8]{0:T(128)}, u32[]{:S(2)}) copy-start(f32[8]{0:T(128)} %param.15) | copy-start | bytes 100
  49.6 7.1 %copy-start.5 = (f32[8,128,128]{2,1,0:T(8,128)S(1)}, f32[8,128,128]{2,1,0:T(8,128)}, u32[]{:S(2)}) copy-start(f32[8,128,128]{2,1,0:T(8,128)} %bitcast_dynamic-update-slice_fusion.7) | copy-start | bytes 1572868
  49.7 7.1 %copy-start.11 = (s32[128,128]{1,0:T(8,128)S(1)}, s32[128,128]{1,0:T(8,128)}, u32[]{:S(2)}) copy-start(s32[128,128]{1,0:T(8,128)} %param.12) | copy-start | bytes 196612
  57.0 55.5 %collective-permute-start.4 = (f32[8,128,8]{2,1,0:T(8,128)S(1)}, f32[8,128,8]{2,1,0:T(8,128)S(1)}, u32[]{:S(2)}, u32[]{:S(2)}) collective-permute-start(f32[8,128,8]{2,1,0:T(8,128)S(1)} %get-tuple-element.33), channel_id=1, source_target_pairs={{0,32},{32,64},{64,96},{96,128},{128,160},{160,192},{192,224},{224... | collective-permute-start | bytes 98312 | tf_op jit(solution)/shard_map/ppermute | solution.py:48
  58.9 53.5 %collective-permute-start.5 = (f32[8,128,8]{2,1,0:T(8,128)S(1)}, f32[8,128,8]{2,1,0:T(8,128)S(1)}, u32[]{:S(2)}, u32[]{:S(2)}) collective-permute-start(f32[8,128,8]{2,1,0:T(8,128)S(1)} %get-tuple-element.34), channel_id=1, source_target_pairs={{32,0},{64,32},{96,64},{128,96},{160,128},{192,160},{224,192},{256... | collective-permute-start | bytes 98312 | tf_op jit(solution)/shard_map/ppermute | solution.py:51
  112.6 9.2 %collective-permute-start.6 = (f32[8,8,144]{2,1,0:T(8,128)S(1)}, f32[8,8,144]{2,1,0:T(8,128)S(1)}, u32[]{:S(2)}, u32[]{:S(2)}) collective-permute-start(f32[8,8,144]{2,1,0:T(8,128)S(1)} %get-tuple-element.23), channel_id=1, source_target_pairs={{0,2},{2,4},{4,6},{6,8},{8,10},{10,12},{12,14},{14,16},{16,18},{18... | collective-permute-start | bytes 110600 | tf_op jit(solution)/shard_map/ppermute | solution.py:48
  114.5 8.6 %collective-permute-start.7 = (f32[8,8,144]{2,1,0:T(8,128)S(1)}, f32[8,8,144]{2,1,0:T(8,128)S(1)}, u32[]{:S(2)}, u32[]{:S(2)}) collective-permute-start(f32[8,8,144]{2,1,0:T(8,128)S(1)} %get-tuple-element.24), channel_id=1, source_target_pairs={{2,0},{4,2},{6,4},{8,6},{10,8},{12,10},{14,12},{16,14},{18,16},{20... | collective-permute-start | bytes 110600 | tf_op jit(solution)/shard_map/ppermute | solution.py:51
  125.3 1.6 %copy-start.4 = (f32[8,128,128]{2,1,0:T(8,128)S(1)}, f32[8,128,128]{2,1,0:T(8,128)}, u32[]{:S(2)}) copy-start(f32[8,128,128]{2,1,0:T(8,128)} %param.8) | copy-start | bytes 1572868
  125.3 1.6 %copy-start.8 = (f32[8,128,128]{2,1,0:T(8,128)S(1)}, f32[8,128,128]{2,1,0:T(8,128)}, u32[]{:S(2)}) copy-start(f32[8,128,128]{2,1,0:T(8,128)} %get-tuple-element.11) | copy-start | bytes 1572868
  125.3 1.5 %copy-start.9 = (f32[8,128,128]{2,1,0:T(8,128)S(1)}, f32[8,128,128]{2,1,0:T(8,128)}, u32[]{:S(2)}) copy-start(f32[8,128,128]{2,1,0:T(8,128)} %get-tuple-element.12) | copy-start | bytes 1572868
where the time goes:
time: 129 us; the launch traced here: 128 us
  starting transfers between devices  49.6 us (38%)
  waiting for transfers between devices  45.5 us (35%)
  other arithmetic  16.5 us (13%)
  local copies, waits for them, and re-layouts  8.49 us (7%)
  blocking collectives  7 us (5%)
    ppermute x2, waiting for transfers between devices, extended(): lax.ppermute(lax.slice_in_dim(block, block.shape[dim] - width, None, axis...  44.1 us
    ppermute x2, starting transfers between devices, extended(): lax.ppermute(lax.slice_in_dim(block, 0, width, axis=dim), axis, backward)  16.6 us
    ppermute x2, starting transfers between devices, with_halo(): lax.ppermute(last, axis, up)  14.6 us
    ppermute x2, starting transfers between devices, with_halo(): lax.ppermute(initial, axis, [(b, a) for a, b in up])  14.5 us
    reduce_sum x1, other arithmetic, on_device(): jnp.sum(thick * active, axis=0)  7.8 us
    all_to_all x1, blocking collectives, copy_for_each(): lax.all_to_all(jnp.broadcast_to(x[None], (count, *x.shape)), axis, 0, 0,...  7 us
    slice x2, local copies, waits for them, and re-layouts, with_halo(): last = lax.slice_in_dim(x, length - width, length, axis=dim)  3.94 us
    ppermute x2, starting transfers between devices, extended(): lax.ppermute(lax.slice_in_dim(block, block.shape[dim] - width, None, axis...  3.84 us
  transfers between devices with their start and end apart: 8, of which 2 were waited for; matrix products, arithmetic and copies ran while one was open for 3% of the time, Pallas kernels for 0%

commit v1 on v0

v1 whole, which is shorter than its diff:
```python
import functools

import jax
import jax.numpy as jnp
from jax import lax
from jax.experimental import pallas as pl
from jax.experimental.pallas import tpu as pltpu
from jax.sharding import PartitionSpec as P

MESH = pl.DeviceIdType.MESH
SUBSTEPS = 4
COURANT = 0.25
VISCOSITY = 0.1
TIMESTEP = SUBSTEPS * COURANT

N = 128
LEVELS = 8
PITCH = 144
PAD = 8
TOP = 16
EXT = 160

HEIGHT, CORIOLIS, DEEPEST, EAST, NORTH, F_EAST, F_NORTH, DEPTH, OCEAN = range(9)
TURNED = (1, 0, 3, 2)


def shift_east(main, side, lane):
    a, b = pltpu.roll(main, N - 1, 1), pltpu.roll(side, N - 1, 1)
    last = lane == N - 1
    return jnp.where(last, b, a), jnp.where(last, a, b)


def shift_west(main, side, lane):
    a, b = pltpu.roll(main, 1, 1), pltpu.roll(side, 1, 1)
    first = lane == 0
    return jnp.where(first, b, a), jnp.where(first, a, b)


def lanes(rows):
    return lax.broadcasted_iota(jnp.int32, (rows, N), 1)


def kernel(
    thick, east_h, north_h, press_h, surf_h, land_h, bottom_h, cor_h,
    base_e, base_n, corr, height_out,
    levels_e, levels_n, levels_p, deep, surf, cor, land, bottom,
    edges, part, part_in, swap, swap_in, late, late_in, totals,
    send1, send2, send_d1, send_d2, recv1, recv2, recv_d1, recv_d2,
    xm, xs, load_sem, send_sem, recv_sem,
):
    gx, gy, gz = lax.axis_index("gx"), lax.axis_index("gy"), lax.axis_index("gz")
    nx, ny = lax.axis_size("gx"), lax.axis_size("gy")
    east, west = lax.rem(gx + 1, nx), lax.rem(gx + nx - 1, nx)
    north, south = lax.rem(gy + 1, ny), lax.rem(gy + ny - 1, ny)
    sister = {"gz": 1 - gz}
    straight = ({"gx": east}, {"gx": west}, {"gy": north}, {"gy": south})
    diagonal = (
        {"gx": east, "gy": north}, {"gx": west, "gy": north},
        {"gx": east, "gy": south}, {"gx": west, "gy": south},
    )

    barrier = pltpu.get_barrier_semaphore()
    for other in (*diagonal, *straight, sister):
        pl.semaphore_signal(barrier, inc=1, device_id=other, device_id_type=MESH)

    loads = []

    def load(source, target):
        copy = pltpu.make_async_copy(source, target, load_sem.at[len(loads)])
        copy.start()
        loads.append(copy)

    load(land_h, land)
    load(bottom_h, bottom)
    load(surf_h, surf)
    load(cor_h, cor)
    levels = (levels_e, levels_n, levels_p)
    for k in range(LEVELS):
        for source, target in zip((east_h, north_h, press_h), levels):
            load(source.at[pl.ds(k * N, N)], target.at[pl.ds(k * PITCH + PAD, N)])

    lane = lanes(8)
    even = (lane & 1) == 0
    left_half = lane < 64
    row = lax.broadcasted_iota(jnp.int32, (8, N), 0)
    first_level = (gz * LEVELS).astype(jnp.float32)
    zero = jnp.zeros((8, N), jnp.float32)

    def by_index(index):
        out = zero
        for k in range(LEVELS):
            out = jnp.where(index == k, thick[k], out)
        return out

    for k in range(4):
        loads[k].wait()
    deep[0:PAD, :] = zero
    deep[PAD + N : PITCH, :] = zero
    deep[PAD : PAD + N, :] = land[...].astype(jnp.float32) * bottom[...].astype(jnp.float32)
    for copy in loads[4:]:
        copy.wait()

    def chunk(i, carry):
        rows = 16
        at = pl.multiple_of(i * rows, rows)
        lane16 = lanes(rows)
        d = deep[pl.ds(at + PAD, rows), :]
        d_e = jnp.where(lane16 == N - 1, 0.0, pltpu.roll(d, N - 1, 1))
        d_w = jnp.where(lane16 == 0, 0.0, pltpu.roll(d, 1, 1))
        d_n = deep[pl.ds(at + PAD + 1, rows), :]
        d_s = deep[pl.ds(at + PAD - 1, rows), :]
        f = cor[pl.ds(at, rows), :]
        sums = [jnp.zeros((rows, N), jnp.float32) for _ in range(4)]
        for k in range(LEVELS):
            level = first_level + k
            here = level < d
            on_e, on_w, on_n, on_s = (level < other for other in (d_e, d_w, d_n, d_s))
            start = k * PITCH + PAD + at

            def around(ref):
                c = ref[pl.ds(start, rows), :]
                e = jnp.where(on_e, pltpu.roll(c, N - 1, 1) - c, 0.0)
                w = jnp.where(on_w, pltpu.roll(c, 1, 1) - c, 0.0)
                n = jnp.where(on_n, ref[pl.ds(start + 1, rows), :] - c, 0.0)
                s = jnp.where(on_s, ref[pl.ds(start - 1, rows), :] - c, 0.0)
                return c, e, w, n, s

            ve, e_e, e_w, e_n, e_s = around(levels_e)
            vn, n_e, n_w, n_n, n_s = around(levels_n)
            _, p_e, p_w, p_n, p_s = around(levels_p)
            tend_e = jnp.where(
                here, 0.5 * (p_w - p_e) + f * vn + VISCOSITY * ((e_e + e_w) + (e_n + e_s)), 0.0
            )
            tend_n = jnp.where(
                here, 0.5 * (p_s - p_n) - f * ve + VISCOSITY * ((n_e + n_w) + (n_n + n_s)), 0.0
            )
            masked_e = jnp.where(here, ve, 0.0)
            masked_n = jnp.where(here, vn, 0.0)
            base_e[pl.ds(k * N + at, rows), :] = masked_e + TIMESTEP * tend_e
            base_n[pl.ds(k * N + at, rows), :] = masked_n + TIMESTEP * tend_n
            weight = thick[k]
            for slot, value in enumerate((masked_e, masked_n, tend_e, tend_n)):
                sums[slot] += weight * value
        for slot in range(4):
            part[slot, pl.ds(at, rows), :] = sums[slot]
        return carry

    lax.fori_loop(0, N // 16, chunk, 0)

    def pack(g, carry):
        carry = list(carry)
        to_east = (lane >> 3) == g
        to_west = (lane >> 3) == lax.rem(g + 1, 16)
        at = pl.multiple_of(g * 8, 8)
        turn = lax.rem(8 * g + 8, N)
        fields = [part.at[slot] for slot in range(4)] + [surf, cor]
        for i, ref in enumerate(fields):
            v = pltpu.roll(ref[pl.ds(at, 8), :], turn, 1)
            carry[i] = jnp.where(to_east, v, carry[i])
            carry[7 + i] = jnp.where(to_west, v, carry[7 + i])
        d = deep[pl.ds(at + PAD, 8), :]
        v = pltpu.roll(d, turn, 1)
        carry[6] = jnp.where(to_east, v, carry[6])
        carry[13] = jnp.where(to_west, v, carry[13])
        pair = (lane - 8 * g) >> 1
        carry[14] = jnp.where(pair == 0, pltpu.roll(d, 8 * g + 1, 1), carry[14])
        for t, ref in enumerate(levels):
            for k in range(LEVELS):
                v = pltpu.roll(ref[pl.ds(at + (k * PITCH + PAD), 8), :], 8 * g + 2 * (k % 4) + 1, 1)
                slot = 15 + 2 * t + k // 4
                carry[slot] = jnp.where(pair == k % 4, v, carry[slot])
        return tuple(carry)

    packed = lax.fori_loop(0, 16, pack, (zero,) * 21)
    to_e, to_w, d_edge, edge = packed[0:7], packed[7:14], packed[14], packed[15:21]
    d_edge = d_edge + pltpu.roll(d_edge, 2, 1)
    d_edge = d_edge + pltpu.roll(d_edge, 4, 1)
    for j in range(6):
        edges[j] = edge[j]
    edges[6] = d_edge
    row_n = [ref[pl.ds(PAD + N - 1, LEVELS, stride=PITCH), :] for ref in levels]
    row_s = [ref[pl.ds(PAD, LEVELS, stride=PITCH), :] for ref in levels]

    def pack_ends(tiles):
        high = low = zero
        for j, v in enumerate(tiles):
            v = pltpu.roll(v, 8 * j + 8, 1)
            high = jnp.where((lane >> 3) == j, v, high)
            low = jnp.where((lane >> 3) == j + 1, v, low)
        return high, low

    rows_e, rows_w = pack_ends([r for t in range(3) for r in (row_n[t], row_s[t])])
    cols_n, cols_s = pack_ends(edge)
    flat = (surf, cor)
    tiles_n = [ref[N - 8 : N, :] for ref in flat] + [deep[PAD + N - 8 : PAD + N, :]]
    tiles_s = [ref[0:8, :] for ref in flat] + [deep[PAD : PAD + 8, :]]
    for i in range(3):
        send1[0, i] = to_e[4 + i]
        send1[1, i] = to_w[4 + i]
        send1[2, i] = tiles_n[i]
        send1[3, i] = tiles_s[i]
    for t in range(3):
        a, b = edge[2 * t], edge[2 * t + 1]
        send1[0, 3 + t] = jnp.where(even, a, pltpu.roll(b, 1, 1))
        send1[1, 3 + t] = jnp.where(even, pltpu.roll(b, N - 1, 1), a)
        send1[2, 3 + t] = row_n[t]
        send1[3, 3 + t] = row_s[t]
    for i, tile in enumerate((rows_e, rows_w, cols_n, cols_s)):
        send1[i, 6] = tile
    corner_n, corner_s = pack_ends(tiles_n), pack_ends(tiles_s)
    for i, tiles in enumerate((
        (rows_e, cols_n, corner_n[0]), (rows_w, cols_n, corner_n[1]),
        (rows_e, cols_s, corner_s[0]), (rows_w, cols_s, corner_s[1]),
    )):
        for j, tile in enumerate(tiles):
            send_d1[i, j] = tile
    for f in range(4):
        swap[f] = to_e[f]
        swap[4 + f] = to_w[f]
        swap[8 + f] = part[f, N - 8 : N, :]
        swap[12 + f] = part[f, 0:8, :]
    swap[16] = by_index(row)

    copies = {}

    def send(name, source, target, slot, other):
        copy = pltpu.make_async_remote_copy(
            src_ref=source, dst_ref=target, send_sem=send_sem.at[slot], recv_sem=recv_sem.at[slot],
            device_id=other, device_id_type=MESH,
        )
        copy.start()
        copies[name] = copy

    pl.semaphore_wait(barrier, 9)
    send("swap", swap, swap_in, 0, sister)
    for i in range(4):
        send(("d1", i), send_d1.at[i], recv_d1.at[3 - i], 3 + i, diagonal[i])
    for i in range(4):
        send(("s1", i), send1.at[i], recv1.at[TURNED[i]], 7 + i, straight[i])
    send("part", part, part_in, 1, sister)

    copies["swap"].wait_recv()
    whole = [swap[j] + swap_in[j] for j in range(16)]
    for i in range(4):
        for f in range(4):
            send2[i, f] = whole[4 * i + f]
    ends_n, ends_s = pack_ends(whole[8:12]), pack_ends(whole[12:16])
    for i, tile in enumerate((*ends_n, *ends_s)):
        send_d2[i] = tile
    for i in range(4):
        send(("d2", i), send_d2.at[i], recv_d2.at[3 - i], 11 + i, diagonal[i])
    for i in range(4):
        send(("s2", i), send2.at[i], recv2.at[TURNED[i]], 15 + i, straight[i])

    upper = gz == 1
    own_thick, other_thick = swap[16], swap_in[16]
    thick_low = jnp.where(upper, other_thick, own_thick)
    thick_high = jnp.where(upper, own_thick, other_thick)

    def depth_of(d):
        out = jnp.zeros_like(d)
        for k in range(2 * LEVELS):
            tile = thick_low if k < LEVELS else thick_high
            weight = jnp.broadcast_to(tile[k % LEVELS : k % LEVELS + 1, :], d.shape)
            out = out + jnp.where(k < d, weight, 0.0)
        return out

    def settle(ref, at, rows):
        d = ref[DEEPEST, pl.ds(at, rows), :]
        ref[DEPTH, pl.ds(at, rows), :] = depth_of(d)
        ref[OCEAN, pl.ds(at, rows), :] = jnp.where(d > 0.0, 1.0, 0.0)

    xm[HEIGHT, TOP : TOP + N, :] = surf[...]
    xm[CORIOLIS, TOP : TOP + N, :] = cor[...]
    xm[DEEPEST, TOP : TOP + N, :] = deep[PAD : PAD + N, :]

    def settle_main(i, carry):
        settle(xm, pl.multiple_of(TOP + 16 * i, 8), 16)
        return carry

    lax.fori_loop(0, N // 16, settle_main, 0)
    copies["part"].wait_recv()
    for f in range(4):
        whole_f = part[f] + part_in[f]
        xm[EAST + f, TOP : TOP + N, :] = whole_f
        if f < 2:
            totals[f] = whole_f

    for i in range(4):
        copies["d1", i].wait_recv()
        copies["s1", i].wait_recv()
    from_e, from_w, from_n, from_s = (recv1.at[i] for i in range(4))

    def beside(tile_e, tile_w, index):
        turn = (N - 8 * (index + 1)) % N if isinstance(index, int) else lax.rem(2 * N - 8 * (index + 1), N)
        return jnp.where(left_half, pltpu.roll(tile_e, turn, 1), pltpu.roll(tile_w, turn, 1))

    for f in range(3):
        xm[f, TOP + N : TOP + N + 8, :] = from_n[f]
        xm[f, TOP - 8 : TOP, :] = from_s[f]
        xs[f, TOP + N : TOP + N + 8, :] = beside(recv_d1[0, 2], recv_d1[1, 2], f)
        xs[f, TOP - 8 : TOP, :] = beside(recv_d1[2, 2], recv_d1[3, 2], f)

    def unpack_inputs(g, carry):
        at = pl.multiple_of(TOP + 8 * g, 8)
        for f in range(3):
            xs[f, pl.ds(at, 8), :] = beside(from_e[f], from_w[f], g)
        return carry

    lax.fori_loop(0, 16, unpack_inputs, 0)

    east_of = lane & 1
    sign = jnp.where(even, -0.5, 0.5)
    in_group = lane & 7

    strip_d = jnp.where(
        in_group == 0, pltpu.roll(from_e[2], N - 8, 1),
        jnp.where(in_group == 1, pltpu.roll(from_w[2], N - 6, 1), 0.0),
    )
    strip_d = strip_d + pltpu.roll(strip_d, 2, 1)
    strip_d = strip_d + pltpu.roll(strip_d, 4, 1)
    own_d = edges[6]
    column_terms = []
    sums_g = sums_e = sums_n = zero
    for half in range(2):
        level_in = (in_group >> 1) + 4 * half
        level = level_in.astype(jnp.float32) + first_level
        both = (level < own_d) & (level < strip_d)
        weight = by_index(level_in)
        diff = []
        for t in range(3):
            if half == 0:
                halo = jnp.where(even, pltpu.roll(from_e[3 + t], N - 1, 1), pltpu.roll(from_w[3 + t], 1, 1))
            else:
                halo = jnp.where(even, from_e[3 + t], from_w[3 + t])
            diff.append(jnp.where(both, halo - edges[2 * t + half], 0.0))
        drag_e, drag_n, grad = VISCOSITY * diff[0], VISCOSITY * diff[1], sign * diff[2]
        column_terms.append((grad + drag_e, drag_n))
        sums_g = sums_g + weight * grad
        sums_e = sums_e + weight * drag_e
        sums_n = sums_n + weight * drag_n

    def over_levels(v):
        v = v + pltpu.roll(v, N - 2, 1)
        return v + pltpu.roll(v, N - 4, 1)

    def swapped(v):
        return jnp.where(even, pltpu.roll(v, N - 1, 1), pltpu.roll(v, 1, 1))

    sums_g, sums_e, sums_n = over_levels(sums_g), over_levels(sums_e), over_levels(sums_n)
    late[0] = jnp.where(
        in_group < 2, sums_g + sums_e,
        jnp.where(
            in_group < 4, pltpu.roll(sums_n, 2, 1),
            jnp.where(
                in_group < 6, pltpu.roll(swapped(sums_g - sums_e), 4, 1), pltpu.roll(swapped(-sums_n), 6, 1)
            ),
        ),
    )

    in_tile = (lane & 15) >> 1
    tile_level = in_tile.astype(jnp.float32) + first_level
    tile_weight = by_index(in_tile) * jnp.where(lane < 32, VISCOSITY, sign)
    for slot, (tile, ahead, behind, corner_at, near, far) in enumerate((
        (from_n[6], recv_d1[0, 1], recv_d1[1, 1], TOP + N, from_n[2], N - 8),
        (from_s[6], recv_d1[2, 1], recv_d1[3, 1], TOP - 8, from_s[2], 0),
    )):
        side = xs[DEEPEST, pl.ds(corner_at, 8), :]

        def ends(v, a, b):
            return jnp.where(
                even, jnp.broadcast_to(v[:, a : a + 1], (8, N)), jnp.broadcast_to(v[:, b : b + 1], (8, N))
            )

        both = (tile_level < ends(near, N - 1, 0)) & (tile_level < ends(side, 0, N - 1))
        halo = jnp.where(even, pltpu.roll(ahead, N - 1, 1), pltpu.roll(behind, 1, 1))
        diff = halo - tile
        if far:
            diff = pltpu.roll(diff, far, 1)
        v = over_levels(jnp.where(both, tile_weight * diff, 0.0))
        late[1 + slot] = v + pltpu.roll(v, N - 8, 1)

    row_level = row.astype(jnp.float32) + first_level
    row_weight = by_index(row)

    def row_pairs(own, halo, d_own, d_halo, factor):
        both = (row_level < d_own) & (row_level < d_halo)
        diff = [jnp.where(both, h - o, 0.0) for h, o in zip(halo, own)]
        return factor * diff[2], VISCOSITY * diff[0], VISCOSITY * diff[1]

    def spread_row(v):
        return jnp.broadcast_to(v, (8, N))

    own_rows_n = [ref[pl.ds(PAD + N - 1, LEVELS, stride=PITCH), :] for ref in levels]
    own_rows_s = [ref[pl.ds(PAD, LEVELS, stride=PITCH), :] for ref in levels]
    main_n = row_pairs(
        own_rows_n, [from_n[3 + t] for t in range(3)],
        spread_row(deep[PAD + N - 1 : PAD + N, :]), spread_row(from_n[2, 0:1, :]), -0.5,
    )
    main_s = row_pairs(
        own_rows_s, [from_s[3 + t] for t in range(3)],
        spread_row(deep[PAD : PAD + 1, :]), spread_row(from_s[2, 7:8, :]), 0.5,
    )
    side_n = row_pairs(
        [beside(from_e[6], from_w[6], 2 * t) for t in range(3)],
        [beside(recv_d1[0, 0], recv_d1[1, 0], 2 * t + 1) for t in range(3)],
        spread_row(xs[DEEPEST, TOP + N - 1 : TOP + N, :]), spread_row(xs[DEEPEST, TOP + N : TOP + N + 1, :]), -0.5,
    )
    side_s = row_pairs(
        [beside(from_e[6], from_w[6], 2 * t + 1) for t in range(3)],
        [beside(recv_d1[2, 0], recv_d1[3, 0], 2 * t) for t in range(3)],
        spread_row(xs[DEEPEST, TOP : TOP + 1, :]), spread_row(xs[DEEPEST, TOP - 1 : TOP, :]), 0.5,
    )
    for slot, pairs in ((3, (main_n, main_s)), (4, (side_n, side_s))):
        tile = zero
        for i, terms in enumerate(pairs):
            for j, term in enumerate(terms):
                total = jnp.sum(row_weight * term, axis=0, keepdims=True)
                tile = jnp.where(row == 3 * i + j, spread_row(total), tile)
        late[slot] = tile
    send("late", late, late_in, 2, sister)

    for at, (grad, drag_e, drag_n) in ((N - 1, main_n), (0, main_s)):
        where_ = pl.ds(at, LEVELS, stride=N)
        base_e[where_, :] = base_e[where_, :] + TIMESTEP * drag_e
        base_n[where_, :] = base_n[where_, :] + TIMESTEP * (grad + drag_n)
    for half in range(2):
        for j in range(2):
            edges[2 * half + j] = TIMESTEP * column_terms[half][j]
    outer = (lane == 0) | (lane == N - 1)

    def add_columns(g, carry):
        for k in range(LEVELS):
            at = pl.multiple_of(g * 8 + k * N, 8)
            turn = (N - 1 - 2 * (k % 4)) - 8 * g
            for j, ref in enumerate((base_e, base_n)):
                v = pltpu.roll(edges[2 * (k // 4) + j], turn, 1)
                ref[pl.ds(at, 8), :] = ref[pl.ds(at, 8), :] + jnp.where(outer, v, 0.0)
        return carry

    lax.fori_loop(0, 16, add_columns, 0)

    def settle_side(i, carry):
        settle(xs, pl.multiple_of(8 + 16 * i, 8), 16)
        return carry

    lax.fori_loop(0, 9, settle_side, 0)
    settle(xm, TOP - 8, 8)
    settle(xm, TOP + N, 8)

    for i in range(4):
        copies["d2", i].wait_recv()
        copies["s2", i].wait_recv()
    for f in range(4):
        xm[EAST + f, TOP + N : TOP + N + 8, :] = recv2[2, f]
        xm[EAST + f, TOP - 8 : TOP, :] = recv2[3, f]
        xs[EAST + f, TOP + N : TOP + N + 8, :] = beside(recv_d2[0], recv_d2[1], f)
        xs[EAST + f, TOP - 8 : TOP, :] = beside(recv_d2[2], recv_d2[3], f)

    copies["late"].wait_recv()
    column_sum = late[0] + late_in[0]

    def unpack_sums(g, carry):
        at = pl.multiple_of(TOP + 8 * g, 8)
        for f in range(2):
            xs[EAST + f, pl.ds(at, 8), :] = beside(recv2[0, f], recv2[1, f], g)
        for f in range(2):
            turn = (N - 1 - 2 * f) - 8 * g
            v = pltpu.roll(column_sum, turn, 1)
            xm[F_EAST + f, pl.ds(at, 8), :] = xm[F_EAST + f, pl.ds(at, 8), :] + jnp.where(outer, v, 0.0)
            v = pltpu.roll(column_sum, turn - 4, 1)
            strip = beside(recv2[0, 2 + f], recv2[1, 2 + f], g)
            xs[F_EAST + f, pl.ds(at, 8), :] = strip + jnp.where(outer, v, 0.0)
        return carry

    lax.fori_loop(0, 16, unpack_sums, 0)

    def add_to(ref, field, at, value):
        ref[field, at, :] = ref[field, at, :] + value

    for slot, at in ((1, pl.ds(TOP + N, 8)), (2, pl.ds(TOP - 8, 8))):
        v = late[slot] + late_in[slot]
        drag_e, drag_n, grad = v, pltpu.roll(v, N - 16, 1), pltpu.roll(v, N - 32, 1)
        add_to(xm, F_EAST, at, jnp.where(outer, pltpu.roll(grad + drag_e, N - 1, 1), 0.0))
        add_to(xm, F_NORTH, at, jnp.where(outer, pltpu.roll(drag_n, N - 1, 1), 0.0))
        add_to(xs, F_EAST, at, jnp.where(outer, pltpu.roll(swapped(grad - drag_e), N - 1, 1), 0.0))
        add_to(xs, F_NORTH, at, jnp.where(outer, pltpu.roll(swapped(-drag_n), N - 1, 1), 0.0))
    for slot, ref in ((3, xm), (4, xs)):
        v = late[slot] + late_in[slot]
        for i, (own, halo) in enumerate(((TOP + N - 1, TOP + N), (TOP, TOP - 1))):
            grad, drag_e, drag_n = (v[3 * i + j : 3 * i + j + 1, :] for j in range(3))
            add_to(ref, F_EAST, pl.ds(own, 1), drag_e)
            add_to(ref, F_NORTH, pl.ds(own, 1), grad + drag_n)
            add_to(ref, F_EAST, pl.ds(halo, 1), -drag_e)
            add_to(ref, F_NORTH, pl.ds(halo, 1), grad - drag_n)

    rows = 48
    lane_r = lanes(rows)
    for step in range(SUBSTEPS):
        for at in range(8, 8 + 3 * rows, rows):
            here = slice(at, at + rows)
            up, down = slice(at + 1, at + rows + 1), slice(at - 1, at + rows - 1)
            main, side = xm[EAST, here, :], xs[EAST, here, :]
            e = shift_east(main, side, lane_r)
            w = shift_west(main, side, lane_r)
            for ref, e_, w_ in ((xm, e[0], w[0]), (xs, e[1], w[1])):
                spread = 0.5 * (e_ - w_) + 0.5 * (ref[NORTH, up, :] - ref[NORTH, down, :])
                ref[HEIGHT, here, :] = ref[OCEAN, here, :] * (ref[HEIGHT, here, :] - COURANT * spread)
        for at in range(8, 8 + 3 * rows, rows):
            here = slice(at, at + rows)
            up, down = slice(at + 1, at + rows + 1), slice(at - 1, at + rows - 1)
            main, side = xm[HEIGHT, here, :], xs[HEIGHT, here, :]
            e = shift_east(main, side, lane_r)
            w = shift_west(main, side, lane_r)
            for ref, e_, w_ in ((xm, e[0], w[0]), (xs, e[1], w[1])):
                if ref is xs and step == SUBSTEPS - 1:
                    continue
                slope_x = 0.5 * (e_ - w_)
                slope_y = 0.5 * (ref[HEIGHT, up, :] - ref[HEIGHT, down, :])
                old_e, old_n = ref[EAST, here, :], ref[NORTH, here, :]
                depth, f, ocean = ref[DEPTH, here, :], ref[CORIOLIS, here, :], ref[OCEAN, here, :]
                ref[EAST, here, :] = ocean * (
                    old_e + COURANT * (-depth * slope_x + f * old_n + ref[F_EAST, here, :])
                )
                ref[NORTH, here, :] = ocean * (
                    old_n + COURANT * (-depth * slope_y - f * old_e + ref[F_NORTH, here, :])
                )

    block = slice(TOP, TOP + N)
    floor_depth = xm[DEPTH, block, :] + (1.0 - xm[OCEAN, block, :])
    for f in range(2):
        corr[f] = (xm[EAST + f, block, :] - totals[f] - TIMESTEP * xm[F_EAST + f, block, :]) / floor_depth
    height_out[...] = xm[HEIGHT, block, :]
    for copy in copies.values():
        copy.wait_send()


def on_device(
    layer_east, layer_north, layer_press, surface, land_sea, bottom_level, coriolis, level_thick
):
    f32 = jnp.float32
    flat = (LEVELS * N, N)
    hbm, vmem = pl.BlockSpec(memory_space=pl.ANY), pl.BlockSpec(memory_space=pltpu.VMEM)
    base_e, base_n, corr, height = pl.pallas_call(
        kernel,
        name="ocean",
        out_shape=(
            jax.ShapeDtypeStruct(flat, f32),
            jax.ShapeDtypeStruct(flat, f32),
            jax.ShapeDtypeStruct((2, N, N), f32),
            jax.ShapeDtypeStruct((N, N), f32),
        ),
        in_specs=[pl.BlockSpec(memory_space=pltpu.SMEM)] + [hbm] * 7,
        out_specs=(vmem,) * 4,
        scratch_shapes=[
            *[pltpu.VMEM((LEVELS * PITCH, N), f32)] * 3,
            pltpu.VMEM((PITCH, N), f32),
            *[pltpu.VMEM((N, N), f32)] * 2,
            *[pltpu.VMEM((N, N), jnp.int32)] * 2,
            pltpu.VMEM((7, 8, N), f32),
            *[pltpu.VMEM((4, N, N), f32)] * 2,
            *[pltpu.VMEM((17, 8, N), f32)] * 2,
            *[pltpu.VMEM((5, 8, N), f32)] * 2,
            pltpu.VMEM((2, N, N), f32),
            *[
                pltpu.VMEM(shape, f32)
                for _ in range(2)
                for shape in ((4, 7, 8, N), (4, 4, 8, N), (4, 3, 8, N), (4, 8, N))
            ],
            *[pltpu.VMEM((9, EXT, N), f32)] * 2,
            pltpu.SemaphoreType.DMA((28,)),
            pltpu.SemaphoreType.DMA((19,)),
            pltpu.SemaphoreType.DMA((19,)),
        ],
        compiler_params=pltpu.CompilerParams(collective_id=0, has_side_effects=True),
    )(
        level_thick,
        layer_east.reshape(flat),
        layer_north.reshape(flat),
        layer_press.reshape(flat),
        surface,
        land_sea,
        bottom_level,
        coriolis,
    )
    deepest = land_sea * bottom_level
    indices = (lax.axis_index("gz") * LEVELS + jnp.arange(LEVELS))[:, None, None]
    active = indices < deepest[None]
    shape = (LEVELS, N, N)
    east_next = jnp.where(active, base_e.reshape(shape) + corr[0], 0.0)
    north_next = jnp.where(active, base_n.reshape(shape) + corr[1], 0.0)
    return height, east_next, north_next


def solution(mesh):
    whole, flat = P("gz", "gy", "gx"), P("gy", "gx")
    return jax.shard_map(
        on_device,
        mesh=mesh,
        in_specs=(whole, whole, whole, flat, flat, flat, flat, P("gz")),
        out_specs=(flat, whole, whole),
        check_vma=False,
    )
```

time: 129 us -> 42.9 us (0.33)
  starting transfers between devices: 49.6 us -> 0 us
  waiting for transfers between devices: 45.5 us -> 0 us
  Pallas kernels: 0 us -> 37.2 us
  other arithmetic: 16.5 us -> 3.25 us
  blocking collectives: 7 us -> 0 us
  local copies, waits for them, and re-layouts: 8.49 us -> 1.52 us
    ppermute x8 -> x0, starting transfers between devices: 49.6 us -> none  [the longest x2 16.6 us: extended(): lax.ppermute(lax.slice_in_dim(block, 0, width, axis=dim), axis, backward)]
    ppermute x8 -> x0, waiting for transfers between devices: 45.5 us -> none  [the longest x2 44.1 us: extended(): lax.ppermute(lax.slice_in_dim(block, block.shape[dim] - width, None, axis...]
    pallas_call x0 -> x1, Pallas kernels: none -> 37.2 us  [on_device(): pl.pallas_call(kernel, name='ocean', out_shape=(jax.ShapeDtypeStruct(flat...]
    reduce_sum x2 -> x0, other arithmetic: 7.84 us -> none  [the longest x1 7.8 us: on_device(): jnp.sum(thick * active, axis=0)]
    all_to_all x1 -> x0, blocking collectives: 7 us -> none  [copy_for_each(): lax.all_to_all(jnp.broadcast_to(x[None], (count, *x.shape)), axis, 0, 0,...]
    slice x4 -> x0, local copies, waits for them, and re-layouts: 4.76 us -> none  [the longest x2 3.94 us: with_halo(): last = lax.slice_in_dim(x, length - width, length, axis=dim)]
    mul x8 -> x1, other arithmetic: 3.61 us -> 0.88 us  [on_device(): deepest = land_sea * bottom_level]
    select_n x0 -> x1, other arithmetic: none -> 2.37 us  [on_device(): north_next = jnp.where(active, base_n.reshape(shape) + corr[1], 0.0)]
  transfers between devices with their start and end apart: 8 -> 0, of which waited for: 2 -> 0; matrix products, arithmetic and copies ran while one was open for 3% -> 0% of each run, Pallas kernels for 0% -> 0%
where the time goes in v1:
time: 42.9 us; the launch traced here: 42.6 us
  Pallas kernels  37.2 us (87%)
  other arithmetic  3.25 us (8%)
  local copies, waits for them, and re-layouts  1.52 us (4%)
  between operations  0.66 us (2%)
    pallas_call x1, Pallas kernels, on_device(): pl.pallas_call(kernel, name='ocean', out_shape=(jax.ShapeDtypeStruct(flat...  37.2 us
    select_n x1, other arithmetic, on_device(): north_next = jnp.where(active, base_n.reshape(shape) + corr[1], 0.0)  2.37 us
    add x1, local copies, waits for them, and re-layouts, on_device(): north_next = jnp.where(active, base_n.reshape(shape) + corr[1], 0.0)  0.88 us
    mul x1, other arithmetic, on_device(): deepest = land_sea * bottom_level  0.88 us

profile of v1, /device:TPU:1, one launch (start us, length us, event | category | flops | bytes accessed | tf_op | source)
XLA Modules:
  0.0 42.6 jit_solution(3041849917662041342)
XLA Ops:
  0.6 0.9 %mul.7 = s32[128,128]{1,0:T(8,128)S(1)} multiply(s32[128,128]{1,0:T(8,128)} %land_h.1, s32[128,128]{1,0:T(8,128)} %bottom_h.1) | non-fusion elementwise | flops 16384 | bytes 196608 | tf_op jit(solution)/shard_map/mul | solution.py:586
  1.5 37.2 %ocean.1 = (f32[1024,128]{1,0:T(8,128)}, f32[1024,128]{1,0:T(8,128)}, f32[2,128,128]{2,1,0:T(8,128)}, f32[128,128]{1,0:T(8,128)}) custom-call(f32[8]{0:T(128)} %thick.1, f32[1024,128]{1,0:T(8,128)} %bitcast.11, f32[1024,128]{1,0:T(8,128)} %bitcast.12, f32[1024,128]{1,0:T(8,128)} %bitcast.13, f32[128,128]{1,0:T(8,128)} %surf_h.1, s32[128,128]{1,0:T(8,128)} %land_h.1, ...), custom_call_target="tpu_custom_call" | custom-call | tf_op jit(solution)/shard_map/ocean/pallas_call | solution.py:544
  38.7 0.9 %slice_bitcast_fusion = (f32[128,128]{1,0:T(8,128)S(1)}, f32[128,128]{1,0:T(8,128)S(1)}) fusion(f32[2,128,128]{2,1,0:T(8,128)} %get-tuple-element.9), kind=kLoop, calls=%fused_computation.2 | loop fusion | bytes 262144 | tf_op jit(solution)/shard_map/add | solution.py:591
  39.6 0.0 copy-start
  39.6 2.4 %compare_select_fusion = (f32[8,128,128]{2,1,0:T(8,128)}, f32[8,128,128]{2,1,0:T(8,128)}) fusion(f32[8,128,128]{2,1,0:T(8,128)} %bitcast.10, f32[128,128]{1,0:T(8,128)S(1)} %get-tuple-element.11, s32[128,128]{1,0:T(8,128)S(1)} %mul.7, s32[8]{0:T(128)S(1)} %iota_add_fusion, f32[8,128,128]{2,1,0:T(8,128)} %bitcast.9, f32[128,128]{1,0:T(8,128)S(1)} %get-tuple-element.12), kind=kLoop, calls=%fused_computation | loop fusion | flops 655360 | bytes 2293792 | tf_op jit(solution)/shard_map/jit(_where)/select_n | solution.py:591
  42.0 0.0 copy-done
  42.0 0.6 %copy.12 = f32[128,128]{1,0:T(8,128)} copy(f32[128,128]{1,0:T(8,128)S(1)} %copy-done) | data formatting | bytes 131072
  (1 shorter events, 0.0 us)
Async XLA Ops:
  39.6 2.4 %copy-start = (f32[128,128]{1,0:T(8,128)S(1)}, f32[128,128]{1,0:T(8,128)}, u32[]{:S(2)}) copy-start(f32[128,128]{1,0:T(8,128)} %get-tuple-element.18) | copy-start | bytes 196612

commit v2 on v1

v2 whole, which is shorter than its diff:
```python
import jax
import jax.numpy as jnp
from jax import lax
from jax.experimental import pallas as pl
from jax.experimental.pallas import tpu as pltpu
from jax.sharding import PartitionSpec as P

MESH = pl.DeviceIdType.MESH
SUBSTEPS = 4
COURANT = 0.25
VISCOSITY = 0.1
TIMESTEP = SUBSTEPS * COURANT
assert TIMESTEP == 1.0
VMEM_LIMIT = 16 * 2**20

N = 128
LEVELS = 8
PITCH = 144
PAD = 8
TOP = 16
EXT = 160

HEIGHT, CORIOLIS, DEEPEST, EAST, NORTH, F_EAST, F_NORTH, DEPTH, OCEAN = range(9)
TURNED = (1, 0, 3, 2)


def shift_east(main, side, lane):
    a, b = pltpu.roll(main, N - 1, 1), pltpu.roll(side, N - 1, 1)
    last = lane == N - 1
    return jnp.where(last, b, a), jnp.where(last, a, b)


def shift_west(main, side, lane):
    a, b = pltpu.roll(main, 1, 1), pltpu.roll(side, 1, 1)
    first = lane == 0
    return jnp.where(first, b, a), jnp.where(first, a, b)


def lanes(rows):
    return lax.broadcasted_iota(jnp.int32, (rows, N), 1)


def kernel(
    thick_h, east_h, north_h, press_h, surf_h, land_h, bottom_h, cor_h,
    base_e, base_n, corr, height_out, deep_out,
    thick, levels_e, levels_n, levels_p, deep, surf, cor, land, bottom,
    edges, part, part_in, swap, swap_in, late, late_in, totals,
    send1, send2, send_d1, send_d2, recv1, recv2, recv_d1, recv_d2,
    xm, xs, load_sem, send_sem, recv_sem,
):
    gx, gy, gz = lax.axis_index("gx"), lax.axis_index("gy"), lax.axis_index("gz")
    nx, ny = lax.axis_size("gx"), lax.axis_size("gy")
    east, west = lax.rem(gx + 1, nx), lax.rem(gx + nx - 1, nx)
    north, south = lax.rem(gy + 1, ny), lax.rem(gy + ny - 1, ny)
    sister = {"gz": 1 - gz}
    straight = ({"gx": east}, {"gx": west}, {"gy": north}, {"gy": south})
    diagonal = (
        {"gx": east, "gy": north}, {"gx": west, "gy": north},
        {"gx": east, "gy": south}, {"gx": west, "gy": south},
    )

    barrier = pltpu.get_barrier_semaphore()
    for other in (*diagonal, *straight, sister):
        pl.semaphore_signal(barrier, inc=1, device_id=other, device_id_type=MESH)

    loads = []

    def load(source, target):
        copy = pltpu.make_async_copy(source, target, load_sem.at[len(loads)])
        copy.start()
        loads.append(copy)

    load(thick_h, thick)
    load(land_h, land)
    load(bottom_h, bottom)
    load(surf_h, surf)
    load(cor_h, cor)
    levels = (levels_e, levels_n, levels_p)
    for source, target in zip((east_h, north_h, press_h), levels):
        for k in range(LEVELS):
            load(source.at[pl.ds(k * N, N)], target.at[pl.ds(k * PITCH + PAD, N)])

    lane = lanes(8)
    even = (lane & 1) == 0
    left_half = lane < 64
    row = lax.broadcasted_iota(jnp.int32, (8, N), 0)
    first_level = (gz * LEVELS).astype(jnp.float32)
    zero = jnp.zeros((8, N), jnp.float32)

    def by_index(index):
        out = zero
        for k in range(LEVELS):
            out = jnp.where(index == k, thick[k], out)
        return out

    for copy in loads[:5]:
        copy.wait()
    deep[0:PAD, :] = zero
    deep[PAD + N : PITCH, :] = zero
    deepest = land[...].astype(jnp.float32) * bottom[...].astype(jnp.float32)
    deep[PAD : PAD + N, :] = deepest
    deep_out[...] = deepest

    def each_group(body, carry=()):
        def trip(i, carry):
            for u in range(4):
                carry = body(4 * i + u, carry)
            return carry

        return lax.fori_loop(0, 4, trip, carry)

    def strips(refs):
        def body(g, carry):
            to_east = (lane >> 3) == g
            to_west = (lane >> 3) == lax.rem(g + 1, 16)
            turn = lax.rem(8 * g + 8, N)
            out = []
            for i, (ref, pad) in enumerate(refs):
                v = pltpu.roll(ref[pl.ds(pl.multiple_of(g * 8 + pad, 8), 8), :], turn, 1)
                out += [jnp.where(to_east, v, carry[2 * i]), jnp.where(to_west, v, carry[2 * i + 1])]
            return tuple(out)

        tiles = each_group(body, (zero,) * (2 * len(refs)))
        return tiles[0::2], tiles[1::2]

    to_e, to_w = strips([(surf, 0), (cor, 0), (deep, PAD)])

    def pack_deepest(g, d_edge):
        v = pltpu.roll(deep[pl.ds(pl.multiple_of(g * 8 + PAD, 8), 8), :], 8 * g + 1, 1)
        return jnp.where(((lane - 8 * g) >> 1) == 0, v, d_edge)

    d_edge = each_group(pack_deepest, zero)
    d_edge = d_edge + pltpu.roll(d_edge, 2, 1)
    d_edge = d_edge + pltpu.roll(d_edge, 4, 1)
    edges[6] = d_edge

    edge = []
    for t, ref in enumerate(levels):
        for copy in loads[5 + LEVELS * t : 5 + LEVELS * (t + 1)]:
            copy.wait()

        def pack(g, carry, ref=ref):
            carry = list(carry)
            pair = (lane - 8 * g) >> 1
            for k in range(LEVELS):
                at = pl.multiple_of(g * 8 + (k * PITCH + PAD), 8)
                v = pltpu.roll(ref[pl.ds(at, 8), :], 8 * g + 2 * (k % 4) + 1, 1)
                carry[k // 4] = jnp.where(pair == k % 4, v, carry[k // 4])
            return tuple(carry)

        edge += each_group(pack, (zero, zero))
    for j in range(6):
        edges[j] = edge[j]
    row_n = [ref[pl.ds(PAD + N - 1, LEVELS, stride=PITCH), :] for ref in levels]
    row_s = [ref[pl.ds(PAD, LEVELS, stride=PITCH), :] for ref in levels]

    def pack_ends(tiles):
        high = low = zero
        for j, v in enumerate(tiles):
            v = pltpu.roll(v, 8 * j + 8, 1)
            high = jnp.where((lane >> 3) == j, v, high)
            low = jnp.where((lane >> 3) == j + 1, v, low)
        return high, low

    rows_e, rows_w = pack_ends([r for t in range(3) for r in (row_n[t], row_s[t])])
    cols_n, cols_s = pack_ends(edge)
    flat = (surf, cor)
    tiles_n = [ref[N - 8 : N, :] for ref in flat] + [deep[PAD + N - 8 : PAD + N, :]]
    tiles_s = [ref[0:8, :] for ref in flat] + [deep[PAD : PAD + 8, :]]
    for i in range(3):
        send1[0, i] = to_e[i]
        send1[1, i] = to_w[i]
        send1[2, i] = tiles_n[i]
        send1[3, i] = tiles_s[i]
    for t in range(3):
        a, b = edge[2 * t], edge[2 * t + 1]
        send1[0, 3 + t] = jnp.where(even, a, pltpu.roll(b, 1, 1))
        send1[1, 3 + t] = jnp.where(even, pltpu.roll(b, N - 1, 1), a)
        send1[2, 3 + t] = row_n[t]
        send1[3, 3 + t] = row_s[t]
    for i, tile in enumerate((rows_e, rows_w, cols_n, cols_s)):
        send1[i, 6] = tile
    corner_n, corner_s = pack_ends(tiles_n), pack_ends(tiles_s)
    for i, tiles in enumerate((
        (rows_e, cols_n, corner_n[0]), (rows_w, cols_n, corner_n[1]),
        (rows_e, cols_s, corner_s[0]), (rows_w, cols_s, corner_s[1]),
    )):
        for j, tile in enumerate(tiles):
            send_d1[i, j] = tile
    swap[16] = by_index(row)

    copies = {}

    def send(name, source, target, slot, other):
        copy = pltpu.make_async_remote_copy(
            src_ref=source, dst_ref=target, send_sem=send_sem.at[slot], recv_sem=recv_sem.at[slot],
            device_id=other, device_id_type=MESH,
        )
        copy.start()
        copies[name] = copy

    pl.semaphore_wait(barrier, 9)
    for i in range(4):
        send(("d1", i), send_d1.at[i], recv_d1.at[3 - i], 3 + i, diagonal[i])
    for i in range(4):
        send(("s1", i), send1.at[i], recv1.at[TURNED[i]], 7 + i, straight[i])

    def chunk(i, carry):
        rows = 16
        at = pl.multiple_of(i * rows, rows)
        lane16 = lanes(rows)
        d = deep[pl.ds(at + PAD, rows), :]
        d_e = jnp.where(lane16 == N - 1, 0.0, jnp.minimum(d, pltpu.roll(d, N - 1, 1)))
        d_n = jnp.minimum(d, deep[pl.ds(at + PAD + 1, rows), :])
        d_s = jnp.minimum(d, deep[pl.ds(at + PAD - 1, rows), :])
        f = cor[pl.ds(at, rows), :]
        sums = [jnp.zeros((rows, N), jnp.float32) for _ in range(4)]
        for k in range(LEVELS):
            level = first_level + k
            here, on_e, on_n, on_s = (level < other for other in (d, d_e, d_n, d_s))
            start = k * PITCH + PAD + at

            def around(ref):
                c = ref[pl.ds(start, rows), :]
                e = jnp.where(on_e, pltpu.roll(c, N - 1, 1) - c, 0.0)
                n = jnp.where(on_n, ref[pl.ds(start + 1, rows), :] - c, 0.0)
                s = jnp.where(on_s, c - ref[pl.ds(start - 1, rows), :], 0.0)
                return c, e, pltpu.roll(e, 1, 1), n, s

            ve, e_e, e_w, e_n, e_s = around(levels_e)
            vn, n_e, n_w, n_n, n_s = around(levels_n)
            _, p_e, p_w, p_n, p_s = around(levels_p)
            masked_e = jnp.where(here, ve, 0.0)
            masked_n = jnp.where(here, vn, 0.0)
            tend_e = f * masked_n + VISCOSITY * ((e_e - e_w) + (e_n - e_s)) - 0.5 * (p_e + p_w)
            tend_n = VISCOSITY * ((n_e - n_w) + (n_n - n_s)) - 0.5 * (p_n + p_s) - f * masked_e
            base_e[pl.ds(k * N + at, rows), :] = masked_e + tend_e
            base_n[pl.ds(k * N + at, rows), :] = masked_n + tend_n
            weight = thick[k]
            for slot, value in enumerate((masked_e, masked_n, tend_e, tend_n)):
                sums[slot] += weight * value
        for slot in range(4):
            part[slot, pl.ds(at, rows), :] = sums[slot]
        return carry

    lax.fori_loop(0, N // 16, chunk, 0)
    to_e, to_w = strips([(part.at[slot], 0) for slot in range(4)])
    for f in range(4):
        swap[f] = to_e[f]
        swap[4 + f] = to_w[f]
        swap[8 + f] = part[f, N - 8 : N, :]
        swap[12 + f] = part[f, 0:8, :]
    send("swap", swap, swap_in, 0, sister)
    send("part", part, part_in, 1, sister)

    copies["swap"].wait_recv()
    whole = [swap[j] + swap_in[j] for j in range(16)]
    for i in range(4):
        for f in range(4):
            send2[i, f] = whole[4 * i + f]
    ends_n, ends_s = pack_ends(whole[8:12]), pack_ends(whole[12:16])
    for i, tile in enumerate((*ends_n, *ends_s)):
        send_d2[i] = tile
    for i in range(4):
        send(("d2", i), send_d2.at[i], recv_d2.at[3 - i], 11 + i, diagonal[i])
    for i in range(4):
        send(("s2", i), send2.at[i], recv2.at[TURNED[i]], 15 + i, straight[i])

    upper = gz == 1
    own_thick, other_thick = 0.5 * COURANT * swap[16], 0.5 * COURANT * swap_in[16]
    thick_low = jnp.where(upper, other_thick, own_thick)
    thick_high = jnp.where(upper, own_thick, other_thick)

    def depth_of(d):
        out = jnp.zeros_like(d)
        for k in range(2 * LEVELS):
            tile = thick_low if k < LEVELS else thick_high
            weight = jnp.broadcast_to(tile[k % LEVELS : k % LEVELS + 1, :], d.shape)
            out = out + jnp.where(k < d, weight, 0.0)
        return out

    def settle(ref, at, rows):
        d = ref[DEEPEST, pl.ds(at, rows), :]
        ref[DEPTH, pl.ds(at, rows), :] = depth_of(d)
        ref[OCEAN, pl.ds(at, rows), :] = jnp.where(d > 0.0, 1.0, 0.0)

    xm[HEIGHT, TOP : TOP + N, :] = surf[...]
    xm[CORIOLIS, TOP : TOP + N, :] = COURANT * cor[...]
    xm[DEEPEST, TOP : TOP + N, :] = deep[PAD : PAD + N, :]

    def settle_main(i, carry):
        settle(xm, pl.multiple_of(TOP + 32 * i, 8), 32)
        return carry

    lax.fori_loop(0, N // 32, settle_main, 0)
    copies["part"].wait_recv()
    for f in range(4):
        whole_f = part[f] + part_in[f]
        xm[EAST + f, TOP : TOP + N, :] = whole_f if f < 2 else COURANT * whole_f
        if f < 2:
            totals[f] = whole_f

    for i in range(4):
        copies["d1", i].wait_recv()
        copies["s1", i].wait_recv()
    from_e, from_w, from_n, from_s = (recv1.at[i] for i in range(4))

    def beside(tile_e, tile_w, index):
        turn = (N - 8 * (index + 1)) % N if isinstance(index, int) else lax.rem(2 * N - 8 * (index + 1), N)
        return jnp.where(left_half, pltpu.roll(tile_e, turn, 1), pltpu.roll(tile_w, turn, 1))

    def put(ref, f, at, tile):
        ref[f, at, :] = COURANT * tile if f in (CORIOLIS, F_EAST, F_NORTH) else tile

    beyond_n, beyond_s = pl.ds(TOP + N, 8), pl.ds(TOP - 8, 8)
    d_north = beside(recv_d1[0, 2], recv_d1[1, 2], 2)
    d_south = beside(recv_d1[2, 2], recv_d1[3, 2], 2)
    d_first, d_last = (beside(from_e[2], from_w[2], g) for g in (0, 15))

    east_of = lane & 1
    sign = jnp.where(even, -0.5, 0.5)
    in_group = lane & 7

    strip_d = jnp.where(
        in_group == 0, pltpu.roll(from_e[2], N - 8, 1),
        jnp.where(in_group == 1, pltpu.roll(from_w[2], N - 6, 1), 0.0),
    )
    strip_d = strip_d + pltpu.roll(strip_d, 2, 1)
    strip_d = strip_d + pltpu.roll(strip_d, 4, 1)
    own_d = edges[6]
    column_terms = []
    sums_g = sums_e = sums_n = zero
    for half in range(2):
        level_in = (in_group >> 1) + 4 * half
        level = level_in.astype(jnp.float32) + first_level
        both = (level < own_d) & (level < strip_d)
        weight = by_index(level_in)
        diff = []
        for t in range(3):
            if half == 0:
                halo = jnp.where(even, pltpu.roll(from_e[3 + t], N - 1, 1), pltpu.roll(from_w[3 + t], 1, 1))
            else:
                halo = jnp.where(even, from_e[3 + t], from_w[3 + t])
            diff.append(jnp.where(both, halo - edges[2 * t + half], 0.0))
        drag_e, drag_n, grad = VISCOSITY * diff[0], VISCOSITY * diff[1], sign * diff[2]
        column_terms.append((grad + drag_e, drag_n))
        sums_g = sums_g + weight * grad
        sums_e = sums_e + weight * drag_e
        sums_n = sums_n + weight * drag_n

    def over_levels(v):
        v = v + pltpu.roll(v, N - 2, 1)
        return v + pltpu.roll(v, N - 4, 1)

    def swapped(v):
        return jnp.where(even, pltpu.roll(v, N - 1, 1), pltpu.roll(v, 1, 1))

    sums_g, sums_e, sums_n = over_levels(sums_g), over_levels(sums_e), over_levels(sums_n)
    late[0] = jnp.where(
        in_group < 2, sums_g + sums_e,
        jnp.where(
            in_group < 4, pltpu.roll(sums_n, 2, 1),
            jnp.where(
                in_group < 6, pltpu.roll(swapped(sums_g - sums_e), 4, 1), pltpu.roll(swapped(-sums_n), 6, 1)
            ),
        ),
    )

    in_tile = (lane & 15) >> 1
    tile_level = in_tile.astype(jnp.float32) + first_level
    tile_weight = by_index(in_tile) * jnp.where(lane < 32, VISCOSITY, sign)
    for slot, (tile, ahead, behind, side, near, far) in enumerate((
        (from_n[6], recv_d1[0, 1], recv_d1[1, 1], d_north, from_n[2], N - 8),
        (from_s[6], recv_d1[2, 1], recv_d1[3, 1], d_south, from_s[2], 0),
    )):

        def ends(v, a, b):
            return jnp.where(
                even, jnp.broadcast_to(v[:, a : a + 1], (8, N)), jnp.broadcast_to(v[:, b : b + 1], (8, N))
            )

        both = (tile_level < ends(near, N - 1, 0)) & (tile_level < ends(side, 0, N - 1))
        halo = jnp.where(even, pltpu.roll(ahead, N - 1, 1), pltpu.roll(behind, 1, 1))
        diff = halo - tile
        if far:
            diff = pltpu.roll(diff, far, 1)
        v = over_levels(jnp.where(both, tile_weight * diff, 0.0))
        late[1 + slot] = v + pltpu.roll(v, N - 8, 1)

    row_level = row.astype(jnp.float32) + first_level
    row_weight = by_index(row)

    def row_pairs(own, halo, d_own, d_halo, factor):
        both = (row_level < d_own) & (row_level < d_halo)
        diff = [jnp.where(both, h - o, 0.0) for h, o in zip(halo, own)]
        return factor * diff[2], VISCOSITY * diff[0], VISCOSITY * diff[1]

    def spread_row(v):
        return jnp.broadcast_to(v, (8, N))

    own_rows_n = [ref[pl.ds(PAD + N - 1, LEVELS, stride=PITCH), :] for ref in levels]
    own_rows_s = [ref[pl.ds(PAD, LEVELS, stride=PITCH), :] for ref in levels]
    main_n = row_pairs(
        own_rows_n, [from_n[3 + t] for t in range(3)],
        spread_row(deep[PAD + N - 1 : PAD + N, :]), spread_row(from_n[2, 0:1, :]), -0.5,
    )
    main_s = row_pairs(
        own_rows_s, [from_s[3 + t] for t in range(3)],
        spread_row(deep[PAD : PAD + 1, :]), spread_row(from_s[2, 7:8, :]), 0.5,
    )
    side_n = row_pairs(
        [beside(from_e[6], from_w[6], 2 * t) for t in range(3)],
        [beside(recv_d1[0, 0], recv_d1[1, 0], 2 * t + 1) for t in range(3)],
        spread_row(d_last[7:8, :]), spread_row(d_north[0:1, :]), -0.5,
    )
    side_s = row_pairs(
        [beside(from_e[6], from_w[6], 2 * t + 1) for t in range(3)],
        [beside(recv_d1[2, 0], recv_d1[3, 0], 2 * t) for t in range(3)],
        spread_row(d_first[0:1, :]), spread_row(d_south[7:8, :]), 0.5,
    )
    for slot, pairs in ((3, (main_n, main_s)), (4, (side_n, side_s))):
        tile = zero
        for i, terms in enumerate(pairs):
            for j, term in enumerate(terms):
                total = jnp.sum(row_weight * term, axis=0, keepdims=True)
                tile = jnp.where(row == 3 * i + j, spread_row(total), tile)
        late[slot] = tile
    send("late", late, late_in, 2, sister)

    for at, (grad, drag_e, drag_n) in ((N - 1, main_n), (0, main_s)):
        where_ = pl.ds(at, LEVELS, stride=N)
        base_e[where_, :] = base_e[where_, :] + drag_e
        base_n[where_, :] = base_n[where_, :] + (grad + drag_n)
    for half in range(2):
        for j in range(2):
            edges[2 * half + j] = column_terms[half][j]
    outer = (lane == 0) | (lane == N - 1)

    def add_columns(g, carry):
        for k in range(LEVELS):
            at = pl.multiple_of(g * 8 + k * N, 8)
            turn = (N - 1 - 2 * (k % 4)) - 8 * g
            for j, ref in enumerate((base_e, base_n)):
                v = pltpu.roll(edges[2 * (k // 4) + j], turn, 1)
                ref[pl.ds(at, 8), :] = ref[pl.ds(at, 8), :] + jnp.where(outer, v, 0.0)
        return carry

    for f in range(3):
        put(xm, f, beyond_n, from_n[f])
        put(xm, f, beyond_s, from_s[f])
        put(xs, f, beyond_n, beside(recv_d1[0, 2], recv_d1[1, 2], f))
        put(xs, f, beyond_s, beside(recv_d1[2, 2], recv_d1[3, 2], f))

    def unpack_inputs(g, carry):
        at = pl.multiple_of(TOP + 8 * g, 8)
        for f in range(3):
            put(xs, f, pl.ds(at, 8), beside(from_e[f], from_w[f], g))
        return carry

    each_group(unpack_inputs)
    each_group(add_columns)

    def settle_side(i, carry):
        settle(xs, pl.multiple_of(8 + 48 * i, 8), 48)
        return carry

    lax.fori_loop(0, 3, settle_side, 0)
    settle(xm, TOP - 8, 8)
    settle(xm, TOP + N, 8)

    def add_to(ref, field, at, value):
        ref[field, at, :] = ref[field, at, :] + value

    copies["late"].wait_recv()
    column_sum = COURANT * (late[0] + late_in[0])

    def place_columns(g, carry):
        at = pl.ds(pl.multiple_of(TOP + 8 * g, 8), 8)
        for f in range(2):
            turn = (N - 1 - 2 * f) - 8 * g
            add_to(xm, F_EAST + f, at, jnp.where(outer, pltpu.roll(column_sum, turn, 1), 0.0))
            xs[F_EAST + f, at, :] = jnp.where(outer, pltpu.roll(column_sum, turn - 4, 1), 0.0)
        return carry

    each_group(place_columns)
    for slot, at in ((1, beyond_n), (2, beyond_s)):
        v = COURANT * (late[slot] + late_in[slot])
        drag_e, drag_n, grad = v, pltpu.roll(v, N - 16, 1), pltpu.roll(v, N - 32, 1)
        xm[F_EAST, at, :] = jnp.where(outer, pltpu.roll(grad + drag_e, N - 1, 1), 0.0)
        xm[F_NORTH, at, :] = jnp.where(outer, pltpu.roll(drag_n, N - 1, 1), 0.0)
        xs[F_EAST, at, :] = jnp.where(outer, pltpu.roll(swapped(grad - drag_e), N - 1, 1), 0.0)
        xs[F_NORTH, at, :] = jnp.where(outer, pltpu.roll(swapped(-drag_n), N - 1, 1), 0.0)
    for slot, ref in ((3, xm), (4, xs)):
        v = COURANT * (late[slot] + late_in[slot])
        for i, (own, halo) in enumerate(((TOP + N - 1, TOP + N), (TOP, TOP - 1))):
            grad, drag_e, drag_n = (v[3 * i + j : 3 * i + j + 1, :] for j in range(3))
            add_to(ref, F_EAST, pl.ds(own, 1), drag_e)
            add_to(ref, F_NORTH, pl.ds(own, 1), grad + drag_n)
            add_to(ref, F_EAST, pl.ds(halo, 1), -drag_e)
            add_to(ref, F_NORTH, pl.ds(halo, 1), grad - drag_n)

    for i in range(4):
        copies["d2", i].wait_recv()
        copies["s2", i].wait_recv()

    def put_sum(ref, f, at, tile):
        if f < 2:
            ref[EAST + f, at, :] = tile
        else:
            add_to(ref, EAST + f, at, COURANT * tile)

    for f in range(4):
        put_sum(xm, f, beyond_n, recv2[2, f])
        put_sum(xm, f, beyond_s, recv2[3, f])
        put_sum(xs, f, beyond_n, beside(recv_d2[0], recv_d2[1], f))
        put_sum(xs, f, beyond_s, beside(recv_d2[2], recv_d2[3], f))

    def unpack_sums(g, carry):
        at = pl.ds(pl.multiple_of(TOP + 8 * g, 8), 8)
        for f in range(4):
            put_sum(xs, f, at, beside(recv2[0, f], recv2[1, f], g))
        return carry

    each_group(unpack_sums)

    rows = 48
    lane_r = lanes(rows)
    for step in range(SUBSTEPS):
        for at in range(8, 8 + 3 * rows, rows):
            here = slice(at, at + rows)
            up, down = slice(at + 1, at + rows + 1), slice(at - 1, at + rows - 1)
            main, side = xm[EAST, here, :], xs[EAST, here, :]
            e = shift_east(main, side, lane_r)
            w = shift_west(main, side, lane_r)
            for ref, e_, w_ in ((xm, e[0], w[0]), (xs, e[1], w[1])):
                spread = (e_ - w_) + (ref[NORTH, up, :] - ref[NORTH, down, :])
                ref[HEIGHT, here, :] = ref[OCEAN, here, :] * (ref[HEIGHT, here, :] - (0.5 * COURANT) * spread)
        for at in range(8, 8 + 3 * rows, rows):
            here = slice(at, at + rows)
            up, down = slice(at + 1, at + rows + 1), slice(at - 1, at + rows - 1)
            main, side = xm[HEIGHT, here, :], xs[HEIGHT, here, :]
            e = shift_east(main, side, lane_r)
            w = shift_west(main, side, lane_r)
            for ref, e_, w_ in ((xm, e[0], w[0]), (xs, e[1], w[1])):
                if ref is xs and step == SUBSTEPS - 1:
                    continue
                old_e, old_n = ref[EAST, here, :], ref[NORTH, here, :]
                depth, f = ref[DEPTH, here, :], ref[CORIOLIS, here, :]
                ref[EAST, here, :] = (old_e + ref[F_EAST, here, :]) + (f * old_n - depth * (e_ - w_))
                ref[NORTH, here, :] = (old_n + ref[F_NORTH, here, :]) - (
                    f * old_e + depth * (ref[HEIGHT, up, :] - ref[HEIGHT, down, :])
                )

    block = slice(TOP, TOP + N)
    floor_depth = (2.0 / COURANT) * xm[DEPTH, block, :] + (1.0 - xm[OCEAN, block, :])
    for f in range(2):
        forced = (TIMESTEP / COURANT) * xm[F_EAST + f, block, :]
        corr[f] = (xm[EAST + f, block, :] - totals[f] - forced) / floor_depth
    height_out[...] = xm[HEIGHT, block, :]
    for copy in copies.values():
        copy.wait_send()


def finish(base_e, base_n, corr, height, deep, height_h, east_h, north_h, outs, sem):
    copies = [pltpu.make_async_copy(height, height_h, sem.at[2 * LEVELS])]
    copies[0].start()
    first_level = (lax.axis_index("gz") * LEVELS).astype(jnp.float32)
    for k in range(LEVELS):
        at = pl.ds(k * N, N)
        wet = first_level + k < deep[...]
        for f, (base, target) in enumerate(((base_e, east_h), (base_n, north_h))):
            outs[f, at, :] = jnp.where(wet, base[at, :] + corr[f], 0.0)
            copy = pltpu.make_async_copy(outs.at[f, at], target.at[at], sem.at[2 * k + f])
            copy.start()
            copies.append(copy)
    for copy in copies:
        copy.wait()


def on_device(
    layer_east, layer_north, layer_press, surface, land_sea, bottom_level, coriolis, level_thick
):
    f32 = jnp.float32
    tall = (LEVELS * N, N)
    flat = (N, N)
    hbm, vmem = pl.BlockSpec(memory_space=pltpu.HBM), pl.BlockSpec(memory_space=pltpu.VMEM)
    between = pl.pallas_call(
        kernel,
        name="ocean",
        out_shape=tuple(jax.ShapeDtypeStruct(shape, f32) for shape in (tall, tall, (2, *flat), flat, flat)),
        in_specs=[hbm] * 8,
        out_specs=(vmem,) * 5,
        scratch_shapes=[
            pltpu.SMEM((LEVELS,), f32),
            *[pltpu.VMEM((LEVELS * PITCH, N), f32)] * 3,
            pltpu.VMEM((PITCH, N), f32),
            *[pltpu.VMEM(flat, f32)] * 2,
            *[pltpu.VMEM(flat, jnp.int32)] * 2,
            pltpu.VMEM((7, 8, N), f32),
            *[pltpu.VMEM((4, N, N), f32)] * 2,
            *[pltpu.VMEM((17, 8, N), f32)] * 2,
            *[pltpu.VMEM((5, 8, N), f32)] * 2,
            pltpu.VMEM((2, N, N), f32),
            *[
                pltpu.VMEM(shape, f32)
                for _ in range(2)
                for shape in ((4, 7, 8, N), (4, 4, 8, N), (4, 3, 8, N), (4, 8, N))
            ],
            *[pltpu.VMEM((9, EXT, N), f32)] * 2,
            pltpu.SemaphoreType.DMA((29,)),
            pltpu.SemaphoreType.DMA((19,)),
            pltpu.SemaphoreType.DMA((19,)),
        ],
        compiler_params=pltpu.CompilerParams(
            collective_id=0, has_side_effects=True, vmem_limit_bytes=VMEM_LIMIT
        ),
    )(
        *(
            pltpu.with_memory_space_constraint(x, pltpu.HBM)
            for x in (
                level_thick,
                layer_east.reshape(tall),
                layer_north.reshape(tall),
                layer_press.reshape(tall),
                surface,
                land_sea,
                bottom_level,
                coriolis,
            )
        )
    )
    height, east_next, north_next = pl.pallas_call(
        finish,
        name="finish",
        out_shape=tuple(jax.ShapeDtypeStruct(shape, f32) for shape in (flat, tall, tall)),
        in_specs=[vmem] * 5,
        out_specs=(hbm,) * 3,
        scratch_shapes=[pltpu.VMEM((2, *tall), f32), pltpu.SemaphoreType.DMA((2 * LEVELS + 1,))],
        compiler_params=pltpu.CompilerParams(vmem_limit_bytes=VMEM_LIMIT),
    )(*between)
    shape = (LEVELS, N, N)
    return height, east_next.reshape(shape), north_next.reshape(shape)


def solution(mesh):
    whole, flat = P("gz", "gy", "gx"), P("gy", "gx")
    return jax.shard_map(
        on_device,
        mesh=mesh,
        in_specs=(whole, whole, whole, flat, flat, flat, flat, P("gz")),
        out_specs=(flat, whole, whole),
        check_vma=False,
    )
```

time: 42.9 us -> 34.4 us (0.80)
  Pallas kernels: 37.2 us -> 33.6 us
  other arithmetic: 3.25 us -> 0 us
  local copies, waits for them, and re-layouts: 1.52 us -> 0 us
    pallas_call x1 -> x2, Pallas kernels: 37.2 us -> 33.6 us  [the longest x1 32.5 us: on_device(): pl.pallas_call(kernel, name='ocean', out_shape=tuple((jax.ShapeDtypeStruc...]
    select_n x1 -> x0, other arithmetic: 2.37 us -> none  [on_device(): north_next = jnp.where(active, base_n.reshape(shape) + corr[1], 0.0)]
    add x1 -> x0, local copies, waits for them, and re-layouts: 0.88 us -> none  [on_device(): north_next = jnp.where(active, base_n.reshape(shape) + corr[1], 0.0)]
    mul x1 -> x0, other arithmetic: 0.88 us -> none  [on_device(): deepest = land_sea * bottom_level]
    unnamed x3 -> x0, local copies, waits for them, and re-layouts: 0.63 us -> none
where the time goes in v2:
time: 34.4 us; the launch traced here: 34.3 us
  Pallas kernels  33.6 us (98%)
  between operations  0.64 us (2%)
    pallas_call x1, Pallas kernels, on_device(): pl.pallas_call(kernel, name='ocean', out_shape=tuple((jax.ShapeDtypeStruc...  32.5 us
    pallas_call x1, Pallas kernels, on_device(): pl.pallas_call(finish, name='finish', out_shape=tuple((jax.ShapeDtypeStru...  1.12 us

profile of v2, /device:TPU:1, one launch (start us, length us, event | category | flops | bytes accessed | tf_op | source)
XLA Modules:
  0.0 34.3 jit_solution(16944187865950614660)
XLA Ops:
  0.6 32.5 %ocean.1 = (f32[1024,128]{1,0:T(8,128)S(1)}, f32[1024,128]{1,0:T(8,128)S(1)}, f32[2,128,128]{2,1,0:T(8,128)S(1)}, f32[128,128]{1,0:T(8,128)S(1)}, f32[128,128]{1,0:T(8,128)S(1)}) custom-call(f32[8]{0:T(128)} %thick_h.1, f32[1024,128]{1,0:T(8,128)} %bitcast.5, f32[1024,128]{1,0:T(8,128)} %bitcast.6, f32[1024,128]{1,0:T(8,128)} %bitcast.7, f32[128,128]{1,0:T(8,128)} %surf_h.1, ...), custom_call_target="tpu_custom_call" | custom-call | tf_op jit(solution)/shard_map/ocean/pallas_call | solution.py:587
  33.1 1.1 %finish.1 = (f32[128,128]{1,0:T(8,128)}, f32[1024,128]{1,0:T(8,128)}, f32[1024,128]{1,0:T(8,128)}) custom-call(f32[1024,128]{1,0:T(8,128)S(1)} %get-tuple-element.11.base_e, f32[1024,128]{1,0:T(8,128)S(1)} %get-tuple-element.12.base_n, f32[2,128,128]{2,1,0:T(8,128)S(1)} %get-tuple-element.13.corr, f32[128,128]{1,0:T(8,128)S(1)} %get-tuple-element.14.height, ...), custom_call_target="tpu_custom_call" | custom-call | tf_op jit(solution)/shard_map/finish/pallas_call | solution.py:632
